TPU v7x, 256 devices: a whole 4x4x8 slice. The times are simulated.
256 devices in a mesh: row: 16 (over y, x), col: 16 (over z, core).
Axes of the slice: x: 4, y: 4, z: 8, core: 2. Of those that a mesh axis runs over, the one named last changes fastest.
Arguments:
- fitting: bfloat16 [512, 512, 256], P(('row', 'col')), may hold values from -6 to 6
- coefficients: bfloat16 [64, 64, 6, 256, 128], P('row', 'col'), may hold values from -0.375 to 0.375
- amplitudes: bfloat16 [64, 64, 4096], P('row', 'col'), may hold values from -6 to 6
- intersections: bfloat16 [64, 64, 8, 4096], P('row', 'col'), may hold values from -0.33 to 1.33
- virtual_energy: float32 [64, 64, 64], P('row', 'col'), may hold values from 0.2 to 2
- occupied_energy: float32 [64], replicated, may hold values from -1.5 to -0.3
- kept_count: int32 [64, 64], P('row', 'col'), may hold values from 16 to 64
- orbital_atoms: int32 [64, 3], replicated, may hold values from 0 to 511, as said below
- fock_partner: int32 [64, 4], replicated, may hold values from 0 to 63, as said below
- fock_value: float32 [64, 4], replicated, may hold values from -3 to 3
Outputs:
- residual: float32 [64, 64, 4096], P('row', 'col')
Inputs may be any that keep to these rules, and one draw needn't show every extreme that they name: `orbital_atoms`: the 3 atoms of orbital i are different and lie in [(i // 4) * 32, (i // 4 + 1) * 32). fock_partner[i, n] differs from i by at most 4.
All inputs are finite; a program needn't handle non-finite values.
Results may differ from a plain program's by a relative error of at most 0.0029.
Values may be sent and summed in bfloat16 or wider, within the bound.
A program may use at most 128 MiB of HBM per device.

v0:
```python
import jax
import jax.numpy as jnp
from jax import lax
from jax.sharding import PartitionSpec as P

AUX = 512
NPNO = 64
DOMAIN = 3
PARTNERS = 4


def from_root(value, axis, source):
    kept = jnp.where(lax.axis_index(axis) == source, value, 0).astype(value.dtype)
    return lax.psum(kept, axis)


def passed_along(block, axis, distance):
    devices = range(lax.axis_size(axis))
    route = [(i - distance, i) for i in devices if i - distance in devices]
    return lax.ppermute(block, axis, route)


def on_device(
    fitting,
    coefficients,
    amplitudes,
    intersections,
    virtual_energy,
    occupied_energy,
    kept_count,
    orbital_atoms,
    fock_partner,
    fock_value,
):
    row_count = amplitudes.shape[0]
    column_count = amplitudes.shape[1]
    domain_size = orbital_atoms.shape[1]
    row_place = lax.axis_index("row")
    column_place = lax.axis_index("col")
    row_atoms = fitting.shape[0] * lax.axis_size("col")
    first_row = row_place * row_count
    first_column = column_place * column_count
    wanted = (
        lax.dynamic_slice_in_dim(orbital_atoms, first_row, row_count, 0) - row_place * row_atoms
    )
    piece = lax.all_gather(fitting, "col", axis=0, tiled=True)
    labels = jnp.arange(piece.shape[0], dtype=jnp.int32)
    picker = (wanted[:, :, None] == labels[None, None, :]).astype(jnp.bfloat16)
    added = jnp.einsum("ism,map->isap", picker, piece, preferred_element_type=jnp.float32)
    row_fit = added.astype(jnp.bfloat16)
    source_row = first_column // row_count
    column_fit = from_root(row_fit, "row", source_row)
    own_side = jnp.einsum(
        "isap,ijspq->ijsaq",
        row_fit,
        coefficients[:, :, :domain_size],
        preferred_element_type=jnp.float32,
    ).astype(jnp.bfloat16)
    other_side = jnp.einsum(
        "jsap,ijspq->ijsaq",
        column_fit,
        coefficients[:, :, domain_size:],
        preferred_element_type=jnp.float32,
    ).astype(jnp.bfloat16)
    exchange_part = jnp.einsum(
        "ijsaq,ijsar->ijqr",
        own_side[..., :NPNO],
        own_side[..., NPNO:],
        preferred_element_type=jnp.float32,
    )
    exchange_part = exchange_part + jnp.einsum(
        "ijsaq,ijsar->ijqr",
        other_side[..., :NPNO],
        other_side[..., NPNO:],
        preferred_element_type=jnp.float32,
    )
    exchange_part = exchange_part * (2 * DOMAIN * AUX) ** (-0.5)
    row_partner = lax.dynamic_slice_in_dim(fock_partner, first_row, row_count, 0)
    column_partner = lax.dynamic_slice_in_dim(fock_partner, first_column, column_count, 0)
    below_rows = passed_along(amplitudes, "row", 1)
    above_rows = passed_along(amplitudes, "row", -1)
    row_source = jnp.concatenate([below_rows, amplitudes, above_rows], axis=0)
    below_columns = passed_along(amplitudes, "col", 1)
    above_columns = passed_along(amplitudes, "col", -1)
    column_source = jnp.concatenate([below_columns, amplitudes, above_columns], axis=1)
    row_pick = row_partner - (first_row - column_count)
    column_pick = column_partner - (first_column - column_count)
    from_rows = jnp.transpose(jnp.take(row_source, row_pick, axis=0), (0, 2, 1, 3))
    from_columns = jnp.take(column_source, column_pick, axis=1)
    partners = jnp.concatenate([from_rows, from_columns], axis=2).reshape(
        row_count, column_count, 2 * PARTNERS, NPNO, NPNO
    )
    intersection_mats = intersections.reshape(row_count, column_count, 2 * PARTNERS, NPNO, NPNO)
    half = jnp.einsum(
        "ijnab,ijnbc->ijnac", intersection_mats, partners, preferred_element_type=jnp.float32
    ).astype(jnp.bfloat16)
    sandwich = jnp.einsum(
        "ijnac,ijndc->ijnad", half, intersection_mats, preferred_element_type=jnp.float32
    )
    row_weight = lax.dynamic_slice_in_dim(fock_value, first_row, row_count, 0)
    column_weight = lax.dynamic_slice_in_dim(fock_value, first_column, column_count, 0)
    weights = jnp.concatenate(
        [
            jnp.broadcast_to(row_weight[:, None, :], (row_count, column_count, PARTNERS)),
            jnp.broadcast_to(column_weight[None, :, :], (row_count, column_count, PARTNERS)),
        ],
        axis=2,
    )
    coupling = jnp.einsum("ijn,ijnad->ijad", weights, sandwich)
    row_occupied = lax.dynamic_slice_in_dim(occupied_energy, first_row, row_count, 0)
    column_occupied = lax.dynamic_slice_in_dim(occupied_energy, first_column, column_count, 0)
    shift = (
        virtual_energy[:, :, :, None]
        + virtual_energy[:, :, None, :]
        - row_occupied[:, None, None, None]
        - column_occupied[None, :, None, None]
    )
    current = amplitudes.reshape(row_count, column_count, NPNO, NPNO).astype(jnp.float32)
    result = exchange_part + shift * current - coupling
    levels = jnp.arange(NPNO, dtype=jnp.int32)
    count = kept_count[:, :, None, None]
    keep = (levels[None, None, :, None] < count) & (levels[None, None, None, :] < count)
    masked = jnp.where(keep, result, jnp.zeros_like(result))
    return masked.reshape(row_count, column_count, NPNO * NPNO)


def solution(mesh):
    placed = (
        P(("row", "col"), None, None),
        P("row", "col", None, None, None),
        P("row", "col", None),
        P("row", "col", None, None),
        P("row", "col", None),
        P(),
        P("row", "col"),
        P(),
        P(),
        P(),
    )
    return jax.shard_map(
        on_device, mesh=mesh, in_specs=placed, out_specs=P("row", "col", None), check_vma=False
    )
```

profile of v0, /device:TPU:1, one launch (start us, length us, event | category | flops | bytes accessed | tf_op | source)
XLA Modules:
  0.0 198.9 jit_solution(497864777100827050)
XLA Ops:
  6.5 0.7 all-gather.2.cloned.1.call-update
  7.3 1.0 copy.82
  8.3 4.9 %collective-permute-start.2 = (bf16[4,4,4096]{2,0,1:T(4,128)(2,1)S(1)}, bf16[4,4,4096]{2,0,1:T(4,128)(2,1)S(1)}, u32[]{:S(2)}, u32[]{:S(2)}) collective-permute-start(bf16[4,4,4096]{2,0,1:T(4,128)(2,1)S(1)} %copy.82), channel_id=1, source_target_pairs={{0,1},{1,2},{2,3},{3,4},{4,5},{5,6},{6,7},{7,8},{8,9},{9,10},{10,1... | collective-permute-start | bytes 393224 | tf_op jit(solution)/shard_map/ppermute | solution.py:20
  13.2 1.9 collective-permute-start.3
  15.2 3.1 %collective-permute-start = (bf16[4,4,4096]{2,1,0:T(4,128)(2,1)}, bf16[4,4,4096]{2,1,0:T(4,128)(2,1)S(1)}, u32[]{:S(2)}, u32[]{:S(2)}) collective-permute-start(bf16[4,4,4096]{2,1,0:T(4,128)(2,1)} %param.12), channel_id=1, source_target_pairs={{0,16},{16,32},{32,48},{48,64},{64,80},{80,96},{96,112},{112,128},... | collective-permute-start | bytes 393224 | tf_op jit(solution)/shard_map/ppermute | solution.py:20
  18.3 1.3 collective-permute-start.1
  19.6 0.8 compare_and_fusion.1
  20.8 0.8 dynamic-slice_subtract_fusion
  21.6 0.8 constant_dynamic-slice_fusion.1
  22.4 0.8 iota_compare_fusion
  23.2 6.7 %fusion.63 = (bf16[4,4,3,256,128]{4,3,2,1,0:T(8,128)(2,1)}, bf16[4,4,3,256,128]{4,3,2,1,0:T(8,128)(2,1)}) fusion(bf16[4,4,6,256,128]{4,3,2,1,0:T(8,128)(2,1)} %param.11), kind=kLoop, calls=%fused_computation.53 | loop fusion | bytes 12582912 | tf_op jit(solution)/shard_map/slice | solution.py:62
  30.0 1.0 reshape.47
  31.3 3.3 %reshape.45 = bf16[4,4,8,64,64]{4,3,2,1,0:T(8,128)(2,1)S(1)} reshape(bf16[4,4,8,4096]{3,2,1,0:T(8,128)(2,1)} %param.13) | data formatting | bytes 2097152 | tf_op jit(solution)/shard_map/reshape | solution.py:93
  35.1 1.0 gather_fusion.1
  36.1 0.3 pad_maximum_fusion.1
  36.4 1.8 gather_fusion
  38.2 1.5 fusion.57
  39.7 29.6 %all-gather.2.cloned.1.call-done = bf16[32,512,256]{2,1,0:T(8,128)(2,1)} async-done(((bf16[2,512,256]{2,1,0:T(8,128)(2,1)}), bf16[32,512,256]{2,1,0:T(8,128)(2,1)}) %all-gather.2.cloned.1.call-update) | async-done | bytes 8388624 | tf_op jit(solution)/shard_map/all_gather | solution.py:46
  69.2 12.0 %broadcast_select_fusion = (bf16[4,3,512,256]{3,0,2,1:T(4,128)(2,1)}, bf16[4,3,512,256]{3,0,2,1:T(4,128)(2,1)}) fusion(pred[]{:T(512)S(6)} %eq.19, bf16[32,512,256]{2,1,0:T(8,128)(2,1)} %all-gather.2.cloned.1.call-done, s32[4,3]{0,1:T(4,128)S(1)} %dynamic-slice_subtract_fusion), kind=kOutput, calls=%fused_computation.19 | convolution fusion | flops 103809408 | bytes 14680113 | tf_op jit(solution)/shard_map/ism,map->isap/dot_general | solution.py:49
  81.2 2.0 pad_maximum_fusion
  83.2 3.3 %reshape.44 = bf16[4,4,8,64,64]{4,3,2,1,0:T(8,128)(2,1)} reshape(bf16[4,4,8,4096]{3,2,1,0:T(8,128)(2,1)S(1)} %pad_maximum_fusion) | data formatting | bytes 2097152 | tf_op jit(solution)/shard_map/reshape | solution.py:90
  86.5 5.3 %fusion.18 = bf16[4,4,8,64,64]{4,3,2,1,0:T(8,128)(2,1)} fusion(bf16[4,4,8,64,64]{4,3,2,1,0:T(8,128)(2,1)S(1)} %reshape.45, bf16[4,4,8,64,64]{4,3,2,1,0:T(8,128)(2,1)} %reshape.44), kind=kOutput, calls=%fused_computation.21 | convolution fusion | flops 134742016 | bytes 3145728 | tf_op jit(solution)/shard_map/ijnac,ijndc->ijnad/dot_general | solution.py:97
  91.8 3.8 %fusion.3 = f32[4,4,1,64,64]{4,2,3,1,0:T(1,128)} fusion(f32[4,4,8,1,1]{2,3,4,1,0:T(1,128)S(1)} %bitcast.64, bf16[4,4,8,64,64]{4,3,2,1,0:T(8,128)(2,1)} %fusion.18), kind=kOutput, calls=%fused_computation.7 | convolution fusion | flops 1048576 | bytes 1311232 | tf_op jit(solution)/shard_map/ijn,ijnad->ijad/dot_general | solution.py:109
  95.6 4.8 %convert_bitcast_fusion.1 = bf16[4,4,3,512,128]{3,4,1,2,0:T(8,128)(2,1)S(1)} fusion(bf16[4,4,3,256,128]{4,3,2,1,0:T(8,128)(2,1)} %get-tuple-element.12, bf16[4,3,512,256,1]{3,0,2,1,4:T(4,128)(2,1)} %bitcast.60), kind=kOutput, calls=%fused_computation.6 | convolution fusion | flops 1613758464 | bytes 12582912 | tf_op jit(solution)/shard_map/isap,ijspq->ijsaq/dot_general | solution.py:53
  100.4 0.8 fusion.64
  101.2 1.7 fusion.22
  103.0 82.1 %all-reduce.2.cloned.1.call-done = bf16[4,3,512,256]{3,0,2,1:T(4,128)(2,1)} async-done(((bf16[4,3,512,256]{3,0,2,1:T(4,128)(2,1)}), bf16[4,3,512,256]{3,0,2,1:T(4,128)(2,1)}) %all-reduce.2.cloned.1.call-update) | async-done | bytes 3145744 | tf_op jit(solution)/shard_map/psum | solution.py:14
  185.1 3.7 %convert_bitcast_fusion = bf16[4,4,3,512,128]{3,4,0,2,1:T(8,128)(2,1)S(1)} fusion(bf16[4,4,3,256,128]{4,3,2,1,0:T(8,128)(2,1)S(1)} %copy-done, bf16[4,3,512,256,1]{3,0,2,1,4:T(4,128)(2,1)} %bitcast.59), kind=kOutput, calls=%fused_computation.5 | convolution fusion | flops 1613758464 | bytes 12582912 | tf_op jit(solution)/shard_map/jsap,ijspq->ijsaq/dot_general | solution.py:59
  188.8 0.4 fusion.62
  189.3 0.5 copy-done.2
  190.2 1.0 fusion.52
  191.2 0.9 reshape.46
  (35 shorter events, 1.6 us)
Async XLA Ops:
  6.5 62.7 %all-gather.2.cloned.1.call-start = ((), (), s32[]{:S(2)}) async-start(), calls=%async_computation | async-start | bytes 8912896 | tf_op jit(solution)/shard_map/all_gather | solution.py:46
  7.3 177.8 %all-reduce.2.cloned.1.call-start = ((), (), s32[]{:S(2)}) async-start(), calls=%async_computation.1 | async-start | bytes 6291456 | tf_op jit(solution)/shard_map/psum | solution.py:14
  8.3 26.5 %collective-permute-start.2 = (bf16[4,4,4096]{2,0,1:T(4,128)(2,1)S(1)}, bf16[4,4,4096]{2,0,1:T(4,128)(2,1)S(1)}, u32[]{:S(2)}, u32[]{:S(2)}) collective-permute-start(bf16[4,4,4096]{2,0,1:T(4,128)(2,1)S(1)} %copy.82), channel_id=1, source_target_pairs={{0,1},{1,2},{2,3},{3,4},{4,5},{5,6},{6,7},{7,8},{8,9},{9,10},{10,1... | collective-permute-start | bytes 393224 | tf_op jit(solution)/shard_map/ppermute | solution.py:20
  13.2 21.6 %collective-permute-start.3 = (bf16[4,4,4096]{2,0,1:T(4,128)(2,1)S(1)}, bf16[4,4,4096]{2,0,1:T(4,128)(2,1)S(1)}, u32[]{:S(2)}, u32[]{:S(2)}) collective-permute-start(bf16[4,4,4096]{2,0,1:T(4,128)(2,1)S(1)} %copy.82), channel_id=1, source_target_pairs={{1,0},{2,1},{3,2},{4,3},{5,4},{6,5},{7,6},{8,7},{9,8},{10,9},{11,1... | collective-permute-start | bytes 393224 | tf_op jit(solution)/shard_map/ppermute | solution.py:20
  15.2 20.9 %collective-permute-start = (bf16[4,4,4096]{2,1,0:T(4,128)(2,1)}, bf16[4,4,4096]{2,1,0:T(4,128)(2,1)S(1)}, u32[]{:S(2)}, u32[]{:S(2)}) collective-permute-start(bf16[4,4,4096]{2,1,0:T(4,128)(2,1)} %param.12), channel_id=1, source_target_pairs={{0,16},{16,32},{32,48},{48,64},{64,80},{80,96},{96,112},{112,128},... | collective-permute-start | bytes 393224 | tf_op jit(solution)/shard_map/ppermute | solution.py:20
  18.3 17.8 %collective-permute-start.1 = (bf16[4,4,4096]{2,1,0:T(4,128)(2,1)}, bf16[4,4,4096]{2,1,0:T(4,128)(2,1)S(1)}, u32[]{:S(2)}, u32[]{:S(2)}) collective-permute-start(bf16[4,4,4096]{2,1,0:T(4,128)(2,1)} %param.12), channel_id=1, source_target_pairs={{16,0},{32,16},{48,32},{64,48},{80,64},{96,80},{112,96},{128,112},... | collective-permute-start | bytes 393224 | tf_op jit(solution)/shard_map/ppermute | solution.py:20
  23.2 6.8 %copy-start.4 = (f32[64]{0:T(128)S(1)}, f32[64]{0:T(128)}, u32[]{:S(2)}) copy-start(f32[64]{0:T(128)} %param.15) | copy-start | bytes 772
  23.2 6.8 %copy-start.1 = (bf16[4,4,4096]{2,1,0:T(4,128)(2,1)S(1)}, bf16[4,4,4096]{2,1,0:T(4,128)(2,1)}, u32[]{:S(2)}) copy-start(bf16[4,4,4096]{2,1,0:T(4,128)(2,1)} %param.12) | copy-start | bytes 393220
  101.2 83.8 %copy-start = (bf16[4,4,3,256,128]{4,3,2,1,0:T(8,128)(2,1)S(1)}, bf16[4,4,3,256,128]{4,3,2,1,0:T(8,128)(2,1)}, u32[]{:S(2)}) copy-start(bf16[4,4,3,256,128]{4,3,2,1,0:T(8,128)(2,1)} %get-tuple-element.11) | copy-start | bytes 9437188
  188.8 1.0 copy-start.2
  188.8 1.2 copy-start.3
  188.8 1.2 copy-start.5
  188.8 1.3 copy-start.6
Sparse Core Ops, SparseCore 0:
  9.2 60.0 all-gather.1
  81.4 103.6 all-reduce.1
where the time goes:
time: 199 us
  waiting for transfers between devices  112 us (56%)
  matrix products  32.4 us (16%)
  local copies, waits for them, and re-layouts  22.8 us (11%)
  between operations  13.6 us (7%)
  starting transfers between devices  11.3 us (6%)
  other arithmetic  6.46 us (3%)
    psum x1, waiting for transfers between devices, from_root(): return lax.psum(kept, axis)  82.1 us
    all_gather x1, waiting for transfers between devices, on_device(): piece = lax.all_gather(fitting, 'col', axis=0, tiled=True)  29.6 us
    dot_general x1, matrix products, on_device(): jnp.einsum('ism,map->isap', picker, piece, preferred_element_type=jnp.flo...  12 us
    ppermute x4, starting transfers between devices, passed_along(): return lax.ppermute(block, axis, route)  11.3 us
    slice x1, local copies, waits for them, and re-layouts, on_device(): coefficients[:, :, domain_size:]  6.75 us
    dot_general x1, matrix products, on_device(): jnp.einsum('ijnac,ijndc->ijnad', half, intersection_mats, preferred_eleme...  5.3 us
    dot_general x1, matrix products, on_device(): jnp.einsum('isap,ijspq->ijsaq', row_fit, coefficients[:, :, :domain_size]...  4.82 us
  transfers between devices with their start and end apart: 6, of which 2 were waited for; matrix products, arithmetic and copies ran while one was open for 21% of the time, Pallas kernels for 0%

commit v1 on v0

--- a/solution.py
+++ b/solution.py
@@ -11,7 +11,7 @@
 
 def from_root(value, axis, source):
     kept = jnp.where(lax.axis_index(axis) == source, value, 0).astype(value.dtype)
-    return lax.psum(kept, axis)
+    return jnp.sum(lax.all_gather(kept, axis), axis=0)
 
 
 def passed_along(block, axis, distance):

time: 199 us -> 400 us (2.01)
  waiting for transfers between devices: 112 us -> 298 us
  other arithmetic: 6.46 us -> 21 us
    all_gather x0 -> x1, waiting for transfers between devices: none -> 236 us  [from_root(): return jnp.sum(lax.all_gather(kept, axis), axis=0)]
    psum x1 -> x0, waiting for transfers between devices: 82.1 us -> none  [from_root(): return lax.psum(kept, axis)]
    all_gather x1, waiting for transfers between devices: 29.6 us -> 61.1 us  [on_device(): piece = lax.all_gather(fitting, 'col', axis=0, tiled=True)]
    reduce_sum x0 -> x1, other arithmetic: none -> 16.9 us  [from_root(): return jnp.sum(lax.all_gather(kept, axis), axis=0)]
  transfers between devices with their start and end apart: 6 -> 6, of which waited for: 2 -> 2; matrix products, arithmetic and copies ran while one was open for 21% -> 10% of each run, Pallas kernels for 0% -> 0%
where the time goes in v1:
time: 400 us
  waiting for transfers between devices  298 us (74%)
  matrix products  29.6 us (7%)
  local copies, waits for them, and re-layouts  26.6 us (7%)
  other arithmetic  21 us (5%)
  between operations  13.7 us (3%)
  starting transfers between devices  11.1 us (3%)
    all_gather x1, waiting for transfers between devices, from_root(): return jnp.sum(lax.all_gather(kept, axis), axis=0)  236 us
    all_gather x1, waiting for transfers between devices, on_device(): piece = lax.all_gather(fitting, 'col', axis=0, tiled=True)  61.1 us
    reduce_sum x1, other arithmetic, from_root(): return jnp.sum(lax.all_gather(kept, axis), axis=0)  16.9 us
    dot_general x1, matrix products, on_device(): jnp.einsum('ism,map->isap', picker, piece, preferred_element_type=jnp.flo...  11.1 us
    ppermute x4, starting transfers between devices, passed_along(): return lax.ppermute(block, axis, route)  11 us
  transfers between devices with their start and end apart: 6, of which 2 were waited for; matrix products, arithmetic and copies ran while one was open for 10% of the time, Pallas kernels for 0%

profile of v1, /device:TPU:1, one launch (start us, length us, event | category | flops | bytes accessed | tf_op | source)
XLA Modules:
  0.0 399.7 jit_solution(14663510709073183754)
XLA Ops:
  6.5 0.7 all-gather.4.cloned.1.call-update
  7.3 0.8 dynamic-slice_subtract_fusion
  8.1 61.1 %all-gather.4.cloned.1.call-done = bf16[32,512,256]{2,1,0:T(8,128)(2,1)} async-done(((bf16[2,512,256]{2,1,0:T(8,128)(2,1)}), bf16[32,512,256]{2,1,0:T(8,128)(2,1)}) %all-gather.4.cloned.1.call-update) | async-done | bytes 8388624 | tf_op jit(solution)/shard_map/all_gather | solution.py:46
  69.2 11.1 %broadcast_select_fusion = (bf16[4,3,512,256]{3,0,2,1:T(4,128)(2,1)S(1)}, bf16[4,3,512,256]{3,0,2,1:T(4,128)(2,1)}) fusion(pred[]{:T(512)S(6)} %eq.19, bf16[32,512,256]{2,1,0:T(8,128)(2,1)} %all-gather.4.cloned.1.call-done, s32[4,3]{0,1:T(4,128)S(1)} %dynamic-slice_subtract_fusion), kind=kOutput, calls=%fused_computation.20 | convolution fusion | flops 103809408 | bytes 14680113 | tf_op jit(solution)/shard_map/ism,map->isap/dot_general | solution.py:49
  80.3 2.1 copy.72
  82.4 0.9 copy-done.1
  83.4 2.2 collective-permute-start.3
  85.6 3.4 collective-permute-start.2
  89.0 1.3 collective-permute-start.1
  90.3 4.2 %collective-permute-start = (bf16[4,4,4096]{2,1,0:T(4,128)(2,1)S(1)}, bf16[4,4,4096]{2,1,0:T(4,128)(2,1)S(1)}, u32[]{:S(2)}, u32[]{:S(2)}) collective-permute-start(bf16[4,4,4096]{2,1,0:T(4,128)(2,1)S(1)} %copy-done.1), channel_id=1, source_target_pairs={{0,16},{16,32},{32,48},{48,64},{64,80},{80,96},{96,112},{112,128},... | collective-permute-start | bytes 393224 | tf_op jit(solution)/shard_map/ppermute | solution.py:20
  95.1 7.1 %fusion.63 = (bf16[4,4,3,256,128]{4,3,2,1,0:T(8,128)(2,1)}, bf16[4,4,3,256,128]{4,3,2,1,0:T(8,128)(2,1)}) fusion(bf16[4,4,6,256,128]{4,3,2,1,0:T(8,128)(2,1)} %param.11), kind=kLoop, calls=%fused_computation.54 | loop fusion | bytes 12582912 | tf_op jit(solution)/shard_map/slice | solution.py:62
  102.3 1.0 reshape.47
  103.8 3.3 reshape.45
  107.4 1.0 gather_fusion.1
  108.4 0.3 pad_maximum_fusion.1
  108.7 1.8 gather_fusion
  110.5 0.7 fusion.57
  111.2 1.8 pad_maximum_fusion
  113.0 3.3 reshape.44
  116.3 5.3 %fusion.18 = bf16[4,4,8,64,64]{4,3,2,1,0:T(8,128)(2,1)} fusion(bf16[4,4,8,64,64]{4,3,2,1,0:T(8,128)(2,1)S(1)} %reshape.45, bf16[4,4,8,64,64]{4,3,2,1,0:T(8,128)(2,1)} %reshape.44), kind=kOutput, calls=%fused_computation.22 | convolution fusion | flops 134742016 | bytes 3145728 | tf_op jit(solution)/shard_map/ijnac,ijndc->ijnad/dot_general | solution.py:97
  121.6 3.8 fusion.3
  125.4 4.8 %convert_bitcast_fusion.1 = bf16[4,4,3,512,128]{3,4,1,2,0:T(8,128)(2,1)S(1)} fusion(bf16[4,4,3,256,128]{4,3,2,1,0:T(8,128)(2,1)} %get-tuple-element.12, bf16[4,3,512,256,1]{3,0,2,1,4:T(4,128)(2,1)} %bitcast.64), kind=kOutput, calls=%fused_computation.6 | convolution fusion | flops 1613758464 | bytes 12582912 | tf_op jit(solution)/shard_map/isap,ijspq->ijsaq/dot_general | solution.py:53
  130.2 0.4 fusion.64
  130.7 1.8 fusion.22
  132.4 235.9 %all-gather.6.cloned.1.call-done = bf16[64,3,512,256]{3,2,1,0:T(8,128)(2,1)} async-done(((bf16[4,3,512,256]{3,2,1,0:T(8,128)(2,1)}), bf16[64,3,512,256]{3,2,1,0:T(8,128)(2,1)}) %all-gather.6.cloned.1.call-update) | async-done | bytes 50331664 | tf_op jit(solution)/shard_map/all_gather | solution.py:14
  368.3 16.9 %reduce_sum.12 = bf16[4,3,512,256]{3,2,1,0:T(8,128)(2,1)S(1)} reduce(bf16[16,4,3,512,256]{4,3,2,1,0:T(8,128)(2,1)} %bitcast.62, bf16[]{:T(256)} %constant.60.clone.1), dimensions={0}, to_apply=%region_0.1 | reduce | flops 23592960 | bytes 53477376 | tf_op jit(solution)/shard_map/reduce_sum | solution.py:14
  385.3 2.4 copy.174
  387.7 1.8 convert_bitcast_fusion
  389.6 0.4 fusion.62
  390.1 0.5 copy-done.2
  391.0 1.0 fusion.52
  392.0 0.9 reshape.46
  (44 shorter events, 2.0 us)
Async XLA Ops:
  6.5 62.7 %all-gather.4.cloned.1.call-start = ((), (), s32[]{:S(2)}) async-start(), calls=%async_computation | async-start | bytes 8912896 | tf_op jit(solution)/shard_map/all_gather | solution.py:46
  7.3 361.1 %all-gather.6.cloned.1.call-start = ((), (), s32[]{:S(2)}) async-start(), calls=%async_computation.1 | async-start | bytes 53477376 | tf_op jit(solution)/shard_map/all_gather | solution.py:14
  82.4 0.9 copy-start.1
  82.4 12.1 %copy-start.5 = (s32[64,4]{0,1:T(4,128)S(1)}, s32[64,4]{0,1:T(4,128)}, u32[]{:S(2)}) copy-start(s32[64,4]{0,1:T(4,128)} %param.18) | copy-start | bytes 3076
  82.4 12.5 %copy-start.4 = (f32[64,4]{0,1:T(4,128)S(1)}, f32[64,4]{0,1:T(4,128)}, u32[]{:S(2)}) copy-start(f32[64,4]{0,1:T(4,128)} %param.19) | copy-start | bytes 3076
  82.4 12.6 %copy-start.7 = (s32[4,4]{1,0:T(4,128)S(1)}, s32[4,4]{1,0:T(4,128)}, u32[]{:S(2)}) copy-start(s32[4,4]{1,0:T(4,128)} %param.16) | copy-start | bytes 196
  83.4 23.7 %collective-permute-start.3 = (bf16[4,4,4096]{2,0,1:T(4,128)(2,1)S(1)}, bf16[4,4,4096]{2,0,1:T(4,128)(2,1)S(1)}, u32[]{:S(2)}, u32[]{:S(2)}) collective-permute-start(bf16[4,4,4096]{2,0,1:T(4,128)(2,1)S(1)} %copy.84), channel_id=1, source_target_pairs={{1,0},{2,1},{3,2},{4,3},{5,4},{6,5},{7,6},{8,7},{9,8},{10,9},{11,1... | collective-permute-start | bytes 393224 | tf_op jit(solution)/shard_map/ppermute | solution.py:20
  85.6 21.5 %collective-permute-start.2 = (bf16[4,4,4096]{2,0,1:T(4,128)(2,1)S(1)}, bf16[4,4,4096]{2,0,1:T(4,128)(2,1)S(1)}, u32[]{:S(2)}, u32[]{:S(2)}) collective-permute-start(bf16[4,4,4096]{2,0,1:T(4,128)(2,1)S(1)} %copy.84), channel_id=1, source_target_pairs={{0,1},{1,2},{2,3},{3,4},{4,5},{5,6},{6,7},{7,8},{8,9},{9,10},{10,1... | collective-permute-start | bytes 393224 | tf_op jit(solution)/shard_map/ppermute | solution.py:20
  89.0 19.4 %collective-permute-start.1 = (bf16[4,4,4096]{2,1,0:T(4,128)(2,1)S(1)}, bf16[4,4,4096]{2,1,0:T(4,128)(2,1)S(1)}, u32[]{:S(2)}, u32[]{:S(2)}) collective-permute-start(bf16[4,4,4096]{2,1,0:T(4,128)(2,1)S(1)} %copy-done.1), channel_id=1, source_target_pairs={{16,0},{32,16},{48,32},{64,48},{80,64},{96,80},{112,96},{128,112},... | collective-permute-start | bytes 393224 | tf_op jit(solution)/shard_map/ppermute | solution.py:20
  90.3 18.1 %collective-permute-start = (bf16[4,4,4096]{2,1,0:T(4,128)(2,1)S(1)}, bf16[4,4,4096]{2,1,0:T(4,128)(2,1)S(1)}, u32[]{:S(2)}, u32[]{:S(2)}) collective-permute-start(bf16[4,4,4096]{2,1,0:T(4,128)(2,1)S(1)} %copy-done.1), channel_id=1, source_target_pairs={{0,16},{16,32},{32,48},{48,64},{64,80},{80,96},{96,112},{112,128},... | collective-permute-start | bytes 393224 | tf_op jit(solution)/shard_map/ppermute | solution.py:20
  95.1 7.1 %copy-start.6 = (f32[64]{0:T(128)S(1)}, f32[64]{0:T(128)}, u32[]{:S(2)}) copy-start(f32[64]{0:T(128)} %param.15) | copy-start | bytes 772
  385.3 2.4 copy-start
  389.6 1.0 copy-start.2
  389.6 1.2 copy-start.3
  389.6 1.2 copy-start.8
  389.6 1.3 copy-start.9
Sparse Core Ops, SparseCore 0:
  9.2 60.0 all-gather.3
  82.6 285.7 all-gather.5
